TPU v7x, 128 devices: a whole 4x4x4 slice. The times are simulated.
128 devices in a mesh: fsdp: 8 (over x_lo, y), tp: 16 (over z, x_hi, core).
Axes of the slice: x: 4 (x_hi: 2, x_lo: 2; x = x_hi * 2 + x_lo), y: 4, z: 4, core: 2. Of those that a mesh axis runs over, the one named last changes fastest.
Arguments:
- prefix_states: bfloat16 [32768, 8192], P('fsdp', 'tp'), may hold values from -40 to 40
- new_states: bfloat16 [128, 8192], P('fsdp', 'tp'), may hold values from -40 to 40
- w_query: bfloat16 [8192, 8192], P('tp', 'fsdp'), may hold values from -0.09375 to 0.09375
- w_keyvalue: bfloat16 [8192, 2048], P('tp', 'fsdp'), may hold values from -0.03125 to 0.03125
- w_output: bfloat16 [8192, 8192], P('tp', 'fsdp'), may hold values from -0.25 to 0.25
- lengths: int32 [8, 4], P('fsdp'), may hold values from 1 to 1024, 3072 in all within a row
Outputs:
- kv_cache: bfloat16 [32768, 2048], P('fsdp', 'tp')
- mixed: bfloat16 [128, 8192], P('fsdp', 'tp')
Inputs may be any that keep to these rules, and one draw needn't show every extreme that they name: `lengths`: in every group some sequence has length 1024.
All inputs are finite; a program needn't handle non-finite values.
Results may differ from a plain program's by a relative error of at most 0.02.
Values may be sent and summed in bfloat16 or wider, within the bound.
No kernel may reach another device: no remote copies, remote signals or barrier semaphores. Data moves between devices by JAX's collectives and lax.ppermute only.
A program may use at most 128 MiB of HBM per device.

v0:
```python
import jax
import jax.numpy as jnp
from jax import lax
from jax.experimental import pallas as pl
from jax.experimental.pallas import tpu as pltpu
from jax.sharding import PartitionSpec as P


HD = 128
NSEQ = 4
L = 1024
STEPS = 4
N_FSDP = 8
N_TP = 16
ROWS = NSEQ * STEPS


theta_base = 500000.0
masked_score = -1e30
both = ("fsdp", "tp")
f32 = jnp.float32
bf16 = jnp.bfloat16

Z_FIRST = 2560
Z_TILE = 640


def route(move):
    pairs = []
    for f in range(N_FSDP):
        for t in range(N_TP):
            a, b = move(f, t)
            pairs.append((f * N_TP + t, a * N_TP + b))
    return pairs


def to_core(block):
    return lax.ppermute(block, both, route(lambda f, t: (f, t ^ 1)))


def to_x(block):
    return lax.ppermute(block, both, route(lambda f, t: (f, t ^ 2)))


def to_z(block, step):
    return lax.ppermute(
        block, both, route(lambda f, t: (f, (((t >> 2) + step) % 4) << 2 | (t & 3)))
    )


def to_group(block, flip):
    return lax.ppermute(block, both, route(lambda f, t: (f ^ flip, t)))


def transpose_mesh(block):
    return lax.ppermute(block, both, route(lambda f, t: (t >> 1, 2 * f + (t & 1))))


def output_owner(block):
    return lax.ppermute(
        block, both, route(lambda f, t: ((t >> 3) * 4 + (f & 3), (f >> 2) * 8 + (t & 7)))
    )


def pick_heads(slots, base, messages, merged):
    for j in range(4):
        for k in range(N_FSDP):

            @pl.when(slots[base + j] == k)
            def _():
                merged[:, j * HD : (j + 1) * HD] = messages[k][: merged.shape[0], :]


def product(x1, x2, merged):
    depth = x1.shape[1]
    total = jnp.dot(x1[...], merged[:depth, :], preferred_element_type=f32)
    total = total + jnp.dot(x2[...], merged[depth:, :], preferred_element_type=f32)
    return total.astype(bf16)


def z_kernel(slots, x1, x2, *rest):
    messages, (a0, a1, b0, b1, merged) = rest[:N_FSDP], rest[-5:]
    i = pl.program_id(0)
    a_tiles = pl.num_programs(0) // 2
    region = jnp.where(i >= a_tiles, 1, 0)

    @pl.when((i == 0) | (i == a_tiles))
    def _():
        pick_heads(slots, region * 4, messages, merged)

    total = product(x1, x2, merged)

    @pl.when(region == 0)
    def _():
        a0[...] = total[:, : 2 * HD]
        a1[...] = total[:, 2 * HD :]

    @pl.when(region == 1)
    def _():
        b0[...] = total[:, : 2 * HD]
        b1[...] = total[:, 2 * HD :]


def x_kernel(slots, x1, x2, *rest):
    messages, (far, merged) = rest[:N_FSDP], rest[-2:]

    @pl.when(pl.program_id(0) == 0)
    def _():
        pick_heads(slots, 8, messages, merged)

    far[...] = product(x1, x2, merged)


def x_merge_kernel(slots, x1, x2, *rest):
    messages, rest = rest[:N_FSDP], rest[N_FSDP:]
    addend, w_query, w_keyvalue = rest[:3]
    parts, (terms, merged, rows_ref) = rest[3:11], rest[11:]
    i = pl.program_id(0)

    @pl.when(i == 0)
    def _():
        pick_heads(slots, 8, messages, merged)

    depth = x1.shape[1]
    total = jnp.dot(x1[...], merged[:depth, :], preferred_element_type=f32)
    total = total + jnp.dot(x2[...], merged[depth:, :], preferred_element_type=f32)
    total = (total + addend[...].astype(f32)).astype(bf16)
    for side in range(2):

        @pl.when(i == side)
        def _():
            for j in range(4):
                parts[4 * side + j][...] = total[:, j * HD : (j + 1) * HD]

    @pl.when(i == 1)
    def _():
        fresh_rows(slots[12], messages, w_query, w_keyvalue, terms, rows_ref)


def fresh_rows(group, messages, w_query, w_keyvalue, out, rows_ref):
    for k in range(N_FSDP):
        low = pl.multiple_of((group ^ k) * ROWS, ROWS)
        for j in range(4):
            rows_ref[pl.ds(low, ROWS), j * HD : (j + 1) * HD] = messages[k][
                1024 + j * ROWS : 1024 + (j + 1) * ROWS, :
            ]
    rows = rows_ref[...]
    query = jnp.dot(rows, w_query[...], preferred_element_type=f32)
    keyvalue = jnp.dot(rows, w_keyvalue[...], preferred_element_type=f32)
    for a in range(N_FSDP):
        for h in range(2):
            low = a * ROWS
            out[2 * a + h, :, :512] = query[low : low + ROWS, h * 512 : (h + 1) * 512]
            out[2 * a + h, :, 512:] = keyvalue[low : low + ROWS, h * HD : (h + 1) * HD]


def whole(shape):
    return pl.BlockSpec(shape, lambda i, s: (0,) * len(shape))


def cost(rows, depth):
    return pl.CostEstimate(
        flops=4 * rows * depth * 4 * HD,
        bytes_accessed=2 * (2 * rows * depth + rows * 4 * HD),
        transcendentals=0,
    )


def z_heads(x1, x2, messages, slots, ready=()):
    depth = x1.shape[1]
    half = Z_FIRST // 2
    a_tiles = half // Z_TILE
    x_spec = pl.BlockSpec((Z_TILE, depth), lambda i, s: (i, 0))
    a_spec = pl.BlockSpec((Z_TILE, 2 * HD), lambda i, s: (jnp.minimum(i, a_tiles - 1), 0))
    b_spec = pl.BlockSpec((Z_TILE, 2 * HD), lambda i, s: (jnp.maximum(i - a_tiles, 0), 0))
    return pl.pallas_call(
        z_kernel,
        out_shape=[jax.ShapeDtypeStruct((half, 2 * HD), bf16)] * 4,
        grid_spec=pltpu.PrefetchScalarGridSpec(
            num_scalar_prefetch=1,
            grid=(2 * a_tiles,),
            in_specs=[x_spec, x_spec]
            + [whole(m.shape) for m in messages]
            + [pl.BlockSpec(memory_space=pl.ANY)] * len(ready),
            out_specs=[a_spec, a_spec, b_spec, b_spec],
            scratch_shapes=[pltpu.VMEM((2 * depth, 4 * HD), bf16)],
        ),
        cost_estimate=cost(Z_FIRST, depth),
        name="z_heads",
    )(slots, x1, x2, *messages, *ready)


def x_rows(depth, half):
    return pl.BlockSpec(
        (pl.Element(half), pl.Element(depth)), lambda i, s: (pl.multiple_of(Z_FIRST + half * i, 256), 0)
    )


def x_heads(x1, x2, messages, slots, ready):
    count, depth = x1.shape
    rows = count - Z_FIRST
    half = rows // 2
    return pl.pallas_call(
        x_kernel,
        out_shape=jax.ShapeDtypeStruct((rows, 4 * HD), bf16),
        grid_spec=pltpu.PrefetchScalarGridSpec(
            num_scalar_prefetch=1,
            grid=(2,),
            in_specs=[x_rows(depth, half)] * 2
            + [whole(m.shape) for m in messages]
            + [pl.BlockSpec(memory_space=pl.ANY)] * len(ready),
            out_specs=pl.BlockSpec((half, 4 * HD), lambda i, s: (i, 0)),
            scratch_shapes=[pltpu.VMEM((2 * depth, 4 * HD), bf16)],
        ),
        cost_estimate=cost(rows, depth),
        name="x_heads",
    )(slots, x1, x2, *messages, *ready)


def x_merge(x1, x2, messages, slots, addend, w_query, w_keyvalue):
    count, depth = x1.shape
    rows = count - Z_FIRST
    half = rows // 2
    terms = (N_TP, ROWS, 640)
    return pl.pallas_call(
        x_merge_kernel,
        out_shape=[jax.ShapeDtypeStruct((half, HD), bf16)] * 8
        + [jax.ShapeDtypeStruct(terms, f32)],
        grid_spec=pltpu.PrefetchScalarGridSpec(
            num_scalar_prefetch=1,
            grid=(2,),
            in_specs=[x_rows(depth, half)] * 2
            + [whole(m.shape) for m in messages]
            + [pl.BlockSpec((half, 4 * HD), lambda i, s: (i, 0))]
            + [whole(w_query.shape), whole(w_keyvalue.shape)],
            out_specs=[whole((half, HD))] * 8 + [whole(terms)],
            scratch_shapes=[
                pltpu.VMEM((2 * depth, 4 * HD), bf16),
                pltpu.VMEM((N_FSDP * ROWS, 512), bf16),
            ],
        ),
        cost_estimate=cost(rows, depth),
        name="x_merge",
    )(slots, x1, x2, *messages, addend, w_query, w_keyvalue)


def message_kernel(kind, w_keyvalue, got, new_states, out):
    depth = got.shape[0]
    out[:depth, :] = jnp.where(kind[0] == 0, w_keyvalue[:, :HD], w_keyvalue[:, HD:])
    out[depth : 2 * depth, :] = got[...]
    for j in range(4):
        low = 2 * depth + j * ROWS
        out[low : low + ROWS, :] = new_states[:, j * HD : (j + 1) * HD]


def pack_message(kind, w_keyvalue, got, new_states):
    vmem = pl.BlockSpec(memory_space=pltpu.VMEM)
    return pl.pallas_call(
        message_kernel,
        out_shape=jax.ShapeDtypeStruct((2 * got.shape[0] + 4 * ROWS, HD), bf16),
        in_specs=[pl.BlockSpec(memory_space=pltpu.SMEM)] + [vmem] * 3,
        out_specs=vmem,
        name="pack_message",
    )(kind, w_keyvalue, got, new_states)


def output_kernel(group, mine, other, w0, w1, w2, w3, out):
    low, high = group[0] & 3, group[0] >> 2
    rows = jnp.concatenate([mine[...], other[...]], axis=0)
    for k, weight in enumerate((w0, w1, w2, w3)):
        total = jnp.dot(rows, weight[...], preferred_element_type=f32).astype(bf16)
        for j in range(2):
            for h in range(2):
                at = (high ^ j) * 8 + (low ^ k) * 2 + h
                out[at] = total[j * ROWS : (j + 1) * ROWS, h * 512 : (h + 1) * 512]


def output_terms(group, mine, other, weights):
    vmem = pl.BlockSpec(memory_space=pltpu.VMEM)
    return pl.pallas_call(
        output_kernel,
        out_shape=jax.ShapeDtypeStruct((N_TP, ROWS, 512), bf16),
        in_specs=[pl.BlockSpec(memory_space=pltpu.SMEM)] + [vmem] * 6,
        out_specs=vmem,
        name="output_terms",
    )(group, mine, other, *weights)


def finish_kernel(*refs):
    cosine, sine, out = refs[14:]
    step = 256
    base = 0
    for addends in (refs[:4], refs[4:8], refs[8:11], refs[11:14]):
        count = addends[0].shape[0]
        for low in range(0, count, step):
            rows = slice(low, low + step)
            total = sum(ref[rows, :].astype(f32) for ref in addends)
            at = base + low
            table = slice(at % L, at % L + step)
            total = total * cosine[table, :] + pltpu.roll(total, HD // 2, 1) * sine[table, :]
            out[at : at + step, :] = total.astype(bf16)
        base += count


def finish_cache(pieces, cosine, sine):
    arrays = [block for block, _, _ in pieces] + [cosine, sine]
    specs = [
        pl.BlockSpec((rows, HD), lambda i, at=at: at) for (_, rows, at) in pieces
    ] + [pl.BlockSpec((L, HD), lambda i: (0, 0))] * 2
    return pl.pallas_call(
        finish_kernel,
        grid=(1,),
        out_shape=jax.ShapeDtypeStruct((NSEQ * L, HD), bf16),
        in_specs=specs,
        out_specs=pl.BlockSpec((NSEQ * L, HD), lambda i: (0, 0)),
        name="finish_cache",
    )(*arrays)


def attention_kernel(info, mine, other, fresh_mine, fresh_other, query, out):
    holds_keys = info[NSEQ] == 0
    scale = HD ** (-0.5)
    fresh_keys = jnp.where(holds_keys, fresh_mine[...], fresh_other[...])
    fresh_values = jnp.where(holds_keys, fresh_other[...], fresh_mine[...])
    for s in range(NSEQ):
        part = slice(s * L, (s + 1) * L)
        keys = jnp.where(holds_keys, mine[part, :], other[part, :])
        values = jnp.where(holds_keys, other[part, :], mine[part, :])
        rows = query[s * 16 : (s + 1) * 16, :]
        last = (((1,), (1,)), ((), ()))
        scores = lax.dot_general(rows, keys, last, preferred_element_type=f32) * scale
        slot = lax.broadcasted_iota(jnp.int32, scores.shape, 1)
        scores = jnp.where(slot < info[s], scores, masked_score)
        fresh = lax.dot_general(rows, fresh_keys, last, preferred_element_type=f32) * scale
        row = lax.broadcasted_iota(jnp.int32, fresh.shape, 0)
        column = lax.broadcasted_iota(jnp.int32, fresh.shape, 1)
        step = column - s * STEPS
        live = (step >= 0) & (step <= (row >> 2))
        fresh = jnp.where(live, fresh, masked_score)
        top = jnp.maximum(
            jnp.max(scores, axis=1, keepdims=True), jnp.max(fresh, axis=1, keepdims=True)
        )
        weight = jnp.exp(scores - top)
        fresh_weight = jnp.exp(fresh - top)
        denominator = jnp.sum(weight, axis=1, keepdims=True) + jnp.sum(
            fresh_weight, axis=1, keepdims=True
        )
        numerator = jnp.dot(weight.astype(bf16), values, preferred_element_type=f32)
        numerator = numerator + jnp.dot(
            fresh_weight.astype(bf16), fresh_values, preferred_element_type=f32
        )
        out[s * 16 : (s + 1) * 16, :] = (numerator / denominator).astype(bf16)


def attend(info, mine, other, fresh_mine, fresh_other, query):
    vmem = pl.BlockSpec(memory_space=pltpu.VMEM)
    return pl.pallas_call(
        attention_kernel,
        out_shape=jax.ShapeDtypeStruct((64, HD), bf16),
        in_specs=[pl.BlockSpec(memory_space=pltpu.SMEM)] + [vmem] * 5,
        out_specs=vmem,
        name="attend",
    )(info, mine, other, fresh_mine, fresh_other, query)


def rotate(values, cosine, sine):
    return values * cosine + jnp.roll(values, HD // 2, axis=-1) * sine


def tables(positions):
    half = HD // 2
    frequency = theta_base ** (-2.0 * jnp.arange(half, dtype=f32) / HD)
    angles = positions[:, None] * frequency[None, :]
    cosine, sine = jnp.cos(angles), jnp.sin(angles)
    return jnp.concatenate([cosine, cosine], 1), jnp.concatenate([-sine, sine], 1)


def add(*blocks):
    total = blocks[0].astype(f32)
    for block in blocks[1:]:
        total = total + block.astype(f32)
    return total.astype(bf16)


def reduce_over_z(far_a, far_b, up_a, up_b, down_a, down_b):
    in_far_a = to_z(far_a, 1)
    in_far_b = to_z(far_b, -1)
    in_up_b = to_z(up_b, 1)
    in_down_a = to_z(down_a, -1)
    merged_a = add(up_a, in_far_a)
    merged_b = add(down_b, in_far_b)
    in_up_a = to_z(merged_a, 1)
    in_down_b = to_z(merged_b, -1)
    return in_down_a, in_up_a, in_up_b, in_down_b


def relay(message):
    far = to_group(message, 2)
    beside = to_group(message, 4)
    one = to_group(message, 1)
    three = to_group(message, 3)
    five = to_group(beside, 1)
    seven = to_group(beside, 3)
    six = to_group(far, 4)
    return [message, one, far, three, beside, five, six, seven]


def body(prefix_states, new_states, w_query, w_keyvalue, w_output, lengths):
    group = lax.axis_index("fsdp")
    me = lax.axis_index("tp")
    z, x, core = me >> 2, (me >> 1) & 1, me & 1
    slots = prefix_states.shape[0]
    holds_keys = core == 0

    lower, upper = w_keyvalue[:, :HD], w_keyvalue[:, HD:]
    got = to_core(jnp.where(holds_keys, upper, lower))
    other_states = to_core(prefix_states)
    kind = core.reshape(1).astype(jnp.int32)
    messages = relay(pack_message(kind, w_keyvalue, got, new_states))

    slot_cos, slot_sin = tables(jnp.arange(L, dtype=f32))
    slot_cos = jnp.where(holds_keys, slot_cos, 1.0)
    slot_sin = jnp.where(holds_keys, slot_sin, 0.0)

    def slot_of(z_step, x_flip):
        return (2 * ((z + z_step) % 4) + (x ^ x_flip)) ^ group

    far, up, down, own = ([(r, 0), (r, 1)] for r in (2, 1, 3, 0))
    order = (2, 1, 3, 0)

    def picked(*pairs):
        return jnp.stack([slot_of(*pair) for pair in pairs] + [group]).astype(jnp.int32)

    first = picked(*far, *down, *far, *up, *((r, 1) for r in order))
    second = picked(*up, *own, *down, *own, *((r, 0) for r in order))
    states = (prefix_states, other_states, messages)
    x_away = x_heads(*states, first, (slot_cos, slot_sin))
    x_in = to_x(x_away)
    far_a, down_a, far_b, up_b = z_heads(*states, first)
    up_a, own_a, down_b, own_b = z_heads(*states, second)
    in_down_a, in_up_a, in_up_b, in_down_b = reduce_over_z(
        far_a, far_b, up_a, up_b, down_a, down_b
    )
    *x_parts, terms = x_merge(*states, second, x_in, w_query, w_keyvalue)
    far_xa, up_xa, down_xa, own_xa, far_xb, up_xb, down_xb, own_xb = x_parts
    x_down_a, x_up_a, x_up_b, x_down_b = reduce_over_z(
        far_xa, far_xb, up_xa, up_xb, down_xa, down_xb
    )
    half = Z_FIRST // 2
    half_x = (slots - Z_FIRST) // 2
    x_in_a = to_x(add(own_a[:, HD:], in_down_a[:, HD:], in_up_a[:, HD:]))
    x_in_b = to_x(add(own_b[:, HD:], in_up_b[:, HD:], in_down_b[:, HD:]))
    outputs = [w_output]
    for k in (1, 2, 3):
        outputs.append(to_group(w_output, k))

    fresh = lax.all_to_all(terms, "tp", 0, 0, tiled=True)
    fresh = transpose_mesh(jnp.sum(fresh, axis=0))
    seq_lengths = lengths[0]
    positions = (
        jnp.repeat(seq_lengths, STEPS) + jnp.tile(jnp.arange(STEPS, dtype=jnp.int32), NSEQ)
    ).astype(f32)
    cosine, sine = tables(positions)
    fresh_cos = jnp.where(holds_keys, cosine, 1.0)
    fresh_sin = jnp.where(holds_keys, sine, 0.0)
    fresh_mine = rotate(fresh[:, 512:], fresh_cos, fresh_sin).astype(bf16)
    fresh_other = to_core(fresh_mine)
    query = (
        rotate(fresh[:, :512].reshape(ROWS, 4, HD), cosine[:, None, :], sine[:, None, :])
        .astype(bf16)
        .reshape(4 * ROWS, HD)
    )

    pieces = [(block, half, (0, 0)) for block in (own_a, in_down_a, in_up_a, x_in_a)]
    pieces += [(block, half, (0, 0)) for block in (own_b, in_up_b, in_down_b, x_in_b)]
    pieces += [(block, half_x, (0, 0)) for block in (own_xa, x_down_a, x_up_a)]
    pieces += [(block, half_x, (0, 0)) for block in (own_xb, x_up_b, x_down_b)]
    cache_mine = finish_cache(pieces, slot_cos, slot_sin)
    cache_other = to_core(cache_mine)
    info = jnp.concatenate([seq_lengths, core.reshape(1).astype(jnp.int32)])
    attended = attend(info, cache_mine, cache_other, fresh_mine, fresh_other, query)
    attended = attended.reshape(ROWS, 512)
    beside = to_group(attended, 4)
    output = output_terms(group.reshape(1).astype(jnp.int32), attended, beside, outputs)
    total = jnp.sum(lax.all_to_all(output, "tp", 0, 0, tiled=True).astype(f32), axis=0)
    mixed = output_owner(total.astype(bf16))
    return cache_mine, mixed


def solution(mesh):
    in_specs = (
        P("fsdp", "tp"),
        P("fsdp", "tp"),
        P("tp", "fsdp"),
        P("tp", "fsdp"),
        P("tp", "fsdp"),
        P("fsdp", None),
    )
    out_specs = (P("fsdp", "tp"), P("fsdp", "tp"))
    return jax.shard_map(
        body, mesh=mesh, in_specs=in_specs, out_specs=out_specs, check_vma=False
    )
```

profile of v0, /device:TPU:26, one launch (start us, length us, event | category | flops | bytes accessed | tf_op | source)
XLA Modules:
  0.0 221.7 jit_solution(6040412435871092573)
XLA Ops:
  2.3 6.0 %collective-permute-done.1.got = bf16[512,128]{1,0:T(8,128)(2,1)S(1)} collective-permute-done((bf16[512,128]{1,0:T(8,128)(2,1)S(1)}, bf16[512,128]{1,0:T(8,128)(2,1)S(1)}, u32[]{:S(2)}, u32[]{:S(2)}) %collective-permute-start.1) | collective-permute-done | bytes 131104 | tf_op jit(solution)/shard_map/ppermute | solution.py:38
  12.5 2.9 %collective-permute-start.4 = (bf16[1088,128]{1,0:T(8,128)(2,1)}, bf16[1088,128]{1,0:T(8,128)(2,1)S(1)}, u32[]{:S(2)}, u32[]{:S(2)}) collective-permute-start(bf16[1088,128]{1,0:T(8,128)(2,1)} %pack_message.1.rest_0_), channel_id=1, source_target_pairs={{0,48},{1,49},{2,50},{3,51},{4,52},{5,53},{6,54},{7,55},{8,56},{9,... | collective-permute-start | bytes 835592 | tf_op jit(solution)/shard_map/ppermute | solution.py:52
  15.4 4.3 %collective-permute-done.5.rest_4_ = bf16[1088,128]{1,0:T(8,128)(2,1)S(1)} collective-permute-done((bf16[1088,128]{1,0:T(8,128)(2,1)}, bf16[1088,128]{1,0:T(8,128)(2,1)S(1)}, u32[]{:S(2)}, u32[]{:S(2)}) %collective-permute-start.5) | collective-permute-done | bytes 278560 | tf_op jit(solution)/shard_map/ppermute | solution.py:52
  22.7 3.3 %collective-permute-done.2.rest_1_ = bf16[1088,128]{1,0:T(8,128)(2,1)S(1)} collective-permute-done((bf16[1088,128]{1,0:T(8,128)(2,1)}, bf16[1088,128]{1,0:T(8,128)(2,1)S(1)}, u32[]{:S(2)}, u32[]{:S(2)}) %collective-permute-start.2) | collective-permute-done | bytes 278560 | tf_op jit(solution)/shard_map/ppermute | solution.py:52
  34.1 8.9 %z_heads.3 = (bf16[1280,256]{1,0:T(8,128)(2,1)}, bf16[1280,256]{1,0:T(8,128)(2,1)}, bf16[1280,256]{1,0:T(8,128)(2,1)}, bf16[1280,256]{1,0:T(8,128)(2,1)}) custom-call(s32[13]{0:T(128)} %stack.60.slots, bf16[4096,512]{1,0:T(8,128)(2,1)} %x1.7, bf16[4096,512]{1,0:T(8,128)(2,1)} %collective-permute-done.x2, bf16[1088,128]{1,0:T(8,128)(2,1)} %pack_message.1.rest_0_, ...), custom_call_target="tpu_custom_call" | custom-call | flops 2684354560 | bytes 7864320 | tf_op jit(solution)/shard_map/z_heads/pallas_call | solution.py:176
  43.0 4.0 %collective-permute-start.14 = (bf16[1280,256]{1,0:T(8,128)(2,1)}, bf16[1280,256]{1,0:T(8,128)(2,1)S(1)}, u32[]{:S(2)}, u32[]{:S(2)}) collective-permute-start(bf16[1280,256]{1,0:T(8,128)(2,1)} %get-tuple-element.26), channel_id=1, source_target_pairs={{0,12},{1,13},{2,14},{3,15},{4,0},{5,1},{6,2},{7,3},{8,4},{9,5},{1... | collective-permute-start | bytes 1966088 | tf_op jit(solution)/shard_map/ppermute | solution.py:46
  51.0 6.0 %x_heads.1 = bf16[1536,512]{1,0:T(8,128)(2,1)} custom-call(s32[13]{0:T(128)} %stack.60.slots, bf16[4096,512]{1,0:T(8,128)(2,1)} %x1.7, bf16[4096,512]{1,0:T(8,128)(2,1)} %collective-permute-done.x2, bf16[1088,128]{1,0:T(8,128)(2,1)} %pack_message.1.rest_0_, bf16[1088,128]{1,0:T(8,128)(2,1)} %copy-done.2, bf16[1088,128]{1,0:T(8,128)(2,1)} %copy-done.1, ...), custom_call_target="tpu_custom_call" | custom-call | flops 1610612736 | bytes 4718592 | tf_op jit(solution)/shard_map/x_heads/pallas_call | solution.py:203
  59.4 8.8 %z_heads.2 = (bf16[1280,256]{1,0:T(8,128)(2,1)}, bf16[1280,256]{1,0:T(8,128)(2,1)}, bf16[1280,256]{1,0:T(8,128)(2,1)}, bf16[1280,256]{1,0:T(8,128)(2,1)}) custom-call(s32[13]{0:T(128)} %stack.58.slots, bf16[4096,512]{1,0:T(8,128)(2,1)} %x1.7, bf16[4096,512]{1,0:T(8,128)(2,1)} %collective-permute-done.x2, bf16[1088,128]{1,0:T(8,128)(2,1)} %pack_message.1.rest_0_, ...), custom_call_target="tpu_custom_call" | custom-call | flops 2684354560 | bytes 7864320 | tf_op jit(solution)/shard_map/z_heads/pallas_call | solution.py:176
  69.6 3.3 %collective-permute-start.15 = (bf16[1280,256]{1,0:T(8,128)(2,1)S(1)}, bf16[1280,256]{1,0:T(8,128)(2,1)S(1)}, u32[]{:S(2)}, u32[]{:S(2)}) collective-permute-start(bf16[1280,256]{1,0:T(8,128)(2,1)S(1)} %add_convert_fusion), channel_id=1, source_target_pairs={{0,12},{1,13},{2,14},{3,15},{4,0},{5,1},{6,2},{7,3},{8,4},{9,5},{1... | collective-permute-start | bytes 1966088 | tf_op jit(solution)/shard_map/ppermute | solution.py:46
  74.9 16.0 %collective-permute-done.10 = bf16[1280,256]{1,0:T(8,128)(2,1)S(1)} collective-permute-done((bf16[1280,256]{1,0:T(8,128)(2,1)}, bf16[1280,256]{1,0:T(8,128)(2,1)S(1)}, u32[]{:S(2)}, u32[]{:S(2)}) %collective-permute-start.10) | collective-permute-done | bytes 655392 | tf_op jit(solution)/shard_map/ppermute | solution.py:46
  97.2 7.9 %x_merge.1 = (bf16[768,128]{1,0:T(8,128)(2,1)}, bf16[768,128]{1,0:T(8,128)(2,1)}, bf16[768,128]{1,0:T(8,128)(2,1)}, bf16[768,128]{1,0:T(8,128)(2,1)}, bf16[768,1...) custom-call(s32[13]{0:T(128)} %stack.58.slots, ...), custom_call_target="tpu_custom_call" | custom-call | flops 1610612736 | bytes 4718592 | tf_op jit(solution)/shard_map/x_merge/pallas_call | solution.py:225
  105.2 3.2 %collective-permute-start.22 = (bf16[768,128]{1,0:T(8,128)(2,1)}, bf16[768,128]{1,0:T(8,128)(2,1)S(1)}, u32[]{:S(2)}, u32[]{:S(2)}) collective-permute-start(bf16[768,128]{1,0:T(8,128)(2,1)} %get-tuple-element.34), channel_id=1, source_target_pairs={{0,12},{1,13},{2,14},{3,15},{4,0},{5,1},{6,2},{7,3},{8,4},{9,5},{1... | collective-permute-start | bytes 589832 | tf_op jit(solution)/shard_map/ppermute | solution.py:46
  112.3 3.7 %all-to-all-start = ((f32[16,16,640]{2,1,0:T(8,128)}), f32[16,16,640]{2,1,0:T(8,128)S(1)}, u32[]{:S(2)}, u32[]{:S(2)}) async-start(f32[16,16,640]{2,1,0:T(8,128)} %get-tuple-element.35), calls=%async_computation | async-start | bytes 1310720 | tf_op jit(solution)/shard_map/all_to_all | solution.py:457
  120.1 12.0 %collective-permute-done.19 = bf16[768,128]{1,0:T(8,128)(2,1)S(1)} collective-permute-done((bf16[768,128]{1,0:T(8,128)(2,1)S(1)}, bf16[768,128]{1,0:T(8,128)(2,1)S(1)}, u32[]{:S(2)}, u32[]{:S(2)}) %collective-permute-start.19) | collective-permute-done | bytes 196640 | tf_op jit(solution)/shard_map/ppermute | solution.py:46
  136.0 3.2 %collective-permute-start.30 = (bf16[512,1024]{1,0:T(8,128)(2,1)S(1)}, bf16[512,1024]{1,0:T(8,128)(2,1)}, u32[]{:S(2)}, u32[]{:S(2)}) collective-permute-start(bf16[512,1024]{1,0:T(8,128)(2,1)S(1)} %copy-done.12), channel_id=1, source_target_pairs={{0,48},{1,49},{2,50},{3,51},{4,52},{5,53},{6,54},{7,55},{8,56},{9,... | collective-permute-start | bytes 3145736 | tf_op jit(solution)/shard_map/ppermute | solution.py:52
  140.1 4.0 %finish_cache.1.mine = bf16[4096,128]{1,0:T(8,128)(2,1)} custom-call(bf16[1280,256]{1,0:T(8,128)(2,1)} %get-tuple-element.19.refs_0_, bf16[1280,256]{1,0:T(8,128)(2,1)} %collective-permute-done.9.refs_1_, bf16[1280,256]{1,0:T(8,128)(2,1)} %collective-permute-done.11.refs_2_, bf16[1280,128]{1,0:T(8,128)(2,1)} %copy-done.16, ...), custom_call_target="tpu_custom_call" | custom-call | tf_op jit(solution)/shard_map/finish_cache/pallas_call | solution.py:310
  144.3 4.4 %collective-permute-start.25 = (f32[16,640]{1,0:T(8,128)S(1)}, f32[16,640]{1,0:T(8,128)S(1)}, u32[]{:S(2)}, u32[]{:S(2)}) collective-permute-start(f32[16,640]{1,0:T(8,128)S(1)} %reduce_sum.21), channel_id=1, source_target_pairs={{0,0},{1,1},{2,16},{3,17},{4,32},{5,33},{6,48},{7,49},{8,64},{9,65... | collective-permute-start | bytes 122888 | tf_op jit(solution)/shard_map/ppermute | solution.py:56
  149.3 5.8 %collective-permute-done.25 = f32[16,640]{1,0:T(8,128)S(1)} collective-permute-done((f32[16,640]{1,0:T(8,128)S(1)}, f32[16,640]{1,0:T(8,128)S(1)}, u32[]{:S(2)}, u32[]{:S(2)}) %collective-permute-start.25) | collective-permute-done | bytes 40992 | tf_op jit(solution)/shard_map/ppermute | solution.py:56
  157.0 3.5 %attend.1 = bf16[64,128]{1,0:T(8,128)(2,1)} custom-call(s32[5]{0:T(128)} %pad_add_fusion.info, bf16[4096,128]{1,0:T(8,128)(2,1)} %finish_cache.1.mine, bf16[4096,128]{1,0:T(8,128)(2,1)} %collective-permute-done.24.other, bf16[16,128]{1,0:T(8,128)(2,1)} %copy-done.22, bf16[16,128]{1,0:T(8,128)(2,1)} %copy-done.23, bf16[64,128]{1,0:T(8,128)(2,1)} %fusion.4.query), custom_call_target="tpu_custom_call" | custom-call | tf_op jit(solution)/shard_map/attend/pallas_call | solution.py:357
  162.9 17.2 %collective-permute-done.29.w2 = bf16[512,1024]{1,0:T(8,128)(2,1)} collective-permute-done((bf16[512,1024]{1,0:T(8,128)(2,1)S(1)}, bf16[512,1024]{1,0:T(8,128)(2,1)}, u32[]{:S(2)}, u32[]{:S(2)}) %collective-permute-start.29) | collective-permute-done | bytes 1048608 | tf_op jit(solution)/shard_map/ppermute | solution.py:52
  180.1 4.1 %collective-permute-done.30.w3 = bf16[512,1024]{1,0:T(8,128)(2,1)} collective-permute-done((bf16[512,1024]{1,0:T(8,128)(2,1)S(1)}, bf16[512,1024]{1,0:T(8,128)(2,1)}, u32[]{:S(2)}, u32[]{:S(2)}) %collective-permute-start.30) | collective-permute-done | bytes 1048608 | tf_op jit(solution)/shard_map/ppermute | solution.py:52
  184.9 3.7 %output_terms.1 = bf16[16,16,512]{2,1,0:T(8,128)(2,1)} custom-call(s32[1]{0:T(128)} %bitcast.7.group, bf16[16,512]{1,0:T(8,128)(2,1)} %copy-done.20, bf16[16,512]{1,0:T(8,128)(2,1)} %copy-done.21, bf16[512,1024]{1,0:T(8,128)(2,1)} %w0.1, bf16[512,1024]{1,0:T(8,128)(2,1)} %copy-done.13, bf16[512,1024]{1,0:T(8,128)(2,1)} %collective-permute-done.29.w2, ...), custom_call_target="tpu_custom_call" | custom-call | tf_op jit(solution)/shard_map/output_terms/pallas_call | solution.py:280
  188.6 24.4 %all_to_all.10 = bf16[16,16,512]{2,1,0:T(8,128)(2,1)S(1)} all-to-all(bf16[16,16,512]{2,1,0:T(8,128)(2,1)} %output_terms.1), channel_id=1, replica_groups=mesh['fsdp'=8,'tp'=16] {'tp'}, dimensions={0} | all-to-all | bytes 524288 | tf_op jit(solution)/shard_map/all_to_all | solution.py:485
  215.8 5.2 %collective-permute-done.31 = bf16[16,512]{1,0:T(8,128)(2,1)S(1)} collective-permute-done((bf16[16,512]{1,0:T(8,128)(2,1)S(1)}, bf16[16,512]{1,0:T(8,128)(2,1)S(1)}, u32[]{:S(2)}, u32[]{:S(2)}) %collective-permute-start.31) | collective-permute-done | bytes 16416 | tf_op jit(solution)/shard_map/ppermute | solution.py:60
  (132 shorter events, 54.7 us)
Async XLA Ops:
  0.6 32.7 %collective-permute-start = (bf16[4096,512]{1,0:T(8,128)(2,1)}, bf16[4096,512]{1,0:T(8,128)(2,1)}, u32[]{:S(2)}, u32[]{:S(2)}) collective-permute-start(bf16[4096,512]{1,0:T(8,128)(2,1)} %x1.7), channel_id=1, source_target_pairs={{0,1},{1,0},{2,3},{3,2},{4,5},{5,4},{6,7},{7,6},{8,9},{9,8},{10,11... | collective-permute-start | bytes 12582920 | tf_op jit(solution)/shard_map/ppermute | solution.py:38
  11.3 11.3 %collective-permute-start.3 = (bf16[1088,128]{1,0:T(8,128)(2,1)}, bf16[1088,128]{1,0:T(8,128)(2,1)S(1)}, u32[]{:S(2)}, u32[]{:S(2)}) collective-permute-start(bf16[1088,128]{1,0:T(8,128)(2,1)} %pack_message.1.rest_0_), channel_id=1, source_target_pairs={{0,32},{1,33},{2,34},{3,35},{4,36},{5,37},{6,38},{7,39},{8,40},{9,... | collective-permute-start | bytes 835592 | tf_op jit(solution)/shard_map/ppermute | solution.py:52
  12.5 13.5 %collective-permute-start.2 = (bf16[1088,128]{1,0:T(8,128)(2,1)}, bf16[1088,128]{1,0:T(8,128)(2,1)S(1)}, u32[]{:S(2)}, u32[]{:S(2)}) collective-permute-start(bf16[1088,128]{1,0:T(8,128)(2,1)} %pack_message.1.rest_0_), channel_id=1, source_target_pairs={{0,16},{1,17},{2,18},{3,19},{4,20},{5,21},{6,22},{7,23},{8,24},{9,... | collective-permute-start | bytes 835592 | tf_op jit(solution)/shard_map/ppermute | solution.py:52
  12.5 15.7 %collective-permute-start.4 = (bf16[1088,128]{1,0:T(8,128)(2,1)}, bf16[1088,128]{1,0:T(8,128)(2,1)S(1)}, u32[]{:S(2)}, u32[]{:S(2)}) collective-permute-start(bf16[1088,128]{1,0:T(8,128)(2,1)} %pack_message.1.rest_0_), channel_id=1, source_target_pairs={{0,48},{1,49},{2,50},{3,51},{4,52},{5,53},{6,54},{7,55},{8,56},{9,... | collective-permute-start | bytes 835592 | tf_op jit(solution)/shard_map/ppermute | solution.py:52
  19.6 11.3 %collective-permute-start.6 = (bf16[1088,128]{1,0:T(8,128)(2,1)S(1)}, bf16[1088,128]{1,0:T(8,128)(2,1)S(1)}, u32[]{:S(2)}, u32[]{:S(2)}) collective-permute-start(bf16[1088,128]{1,0:T(8,128)(2,1)S(1)} %collective-permute-done.5.rest_4_), channel_id=1, source_target_pairs={{0,16},{1,17},{2,18},{3,19},{4,20},{5,21},{6,22},{7,23},{8,24},{9,... | collective-permute-start | bytes 835592 | tf_op jit(solution)/shard_map/ppermute | solution.py:52
  43.0 25.3 %collective-permute-start.14 = (bf16[1280,256]{1,0:T(8,128)(2,1)}, bf16[1280,256]{1,0:T(8,128)(2,1)S(1)}, u32[]{:S(2)}, u32[]{:S(2)}) collective-permute-start(bf16[1280,256]{1,0:T(8,128)(2,1)} %get-tuple-element.26), channel_id=1, source_target_pairs={{0,12},{1,13},{2,14},{3,15},{4,0},{5,1},{6,2},{7,3},{8,4},{9,5},{1... | collective-permute-start | bytes 1966088 | tf_op jit(solution)/shard_map/ppermute | solution.py:46
  57.0 39.0 %collective-permute-start.17 = (bf16[1536,512]{1,0:T(8,128)(2,1)}, bf16[1536,512]{1,0:T(8,128)(2,1)S(1)}, u32[]{:S(2)}, u32[]{:S(2)}) collective-permute-start(bf16[1536,512]{1,0:T(8,128)(2,1)} %x_heads.1), channel_id=1, source_target_pairs={{0,2},{1,3},{2,0},{3,1},{4,6},{5,7},{6,4},{7,5},{8,10},{9,11},{10,... | collective-permute-start | bytes 4718600 | tf_op jit(solution)/shard_map/ppermute | solution.py:42
  59.4 33.7 %collective-permute-start.13 = (bf16[1280,256]{1,0:T(8,128)(2,1)}, bf16[1280,256]{1,0:T(8,128)(2,1)S(1)}, u32[]{:S(2)}, u32[]{:S(2)}) collective-permute-start(bf16[1280,256]{1,0:T(8,128)(2,1)} %get-tuple-element.24), channel_id=1, source_target_pairs={{0,4},{1,5},{2,6},{3,7},{4,8},{5,9},{6,10},{7,11},{8,12},{9,13},{1... | collective-permute-start | bytes 1966088 | tf_op jit(solution)/shard_map/ppermute | solution.py:46
  59.4 31.6 %collective-permute-start.10 = (bf16[1280,256]{1,0:T(8,128)(2,1)}, bf16[1280,256]{1,0:T(8,128)(2,1)S(1)}, u32[]{:S(2)}, u32[]{:S(2)}) collective-permute-start(bf16[1280,256]{1,0:T(8,128)(2,1)} %get-tuple-element.22), channel_id=1, source_target_pairs={{0,4},{1,5},{2,6},{3,7},{4,8},{5,9},{6,10},{7,11},{8,12},{9,13},{1... | collective-permute-start | bytes 1966088 | tf_op jit(solution)/shard_map/ppermute | solution.py:46
  69.6 23.6 %collective-permute-start.15 = (bf16[1280,256]{1,0:T(8,128)(2,1)S(1)}, bf16[1280,256]{1,0:T(8,128)(2,1)S(1)}, u32[]{:S(2)}, u32[]{:S(2)}) collective-permute-start(bf16[1280,256]{1,0:T(8,128)(2,1)S(1)} %add_convert_fusion), channel_id=1, source_target_pairs={{0,12},{1,13},{2,14},{3,15},{4,0},{5,1},{6,2},{7,3},{8,4},{9,5},{1... | collective-permute-start | bytes 1966088 | tf_op jit(solution)/shard_map/ppermute | solution.py:46
  72.9 35.5 %collective-permute-start.9 = (bf16[1280,256]{1,0:T(8,128)(2,1)}, bf16[1280,256]{1,0:T(8,128)(2,1)}, u32[]{:S(2)}, u32[]{:S(2)}) collective-permute-start(bf16[1280,256]{1,0:T(8,128)(2,1)} %get-tuple-element.20), channel_id=1, source_target_pairs={{0,12},{1,13},{2,14},{3,15},{4,0},{5,1},{6,2},{7,3},{8,4},{9,5},{1... | collective-permute-start | bytes 1966088 | tf_op jit(solution)/shard_map/ppermute | solution.py:46
  93.1 16.6 %collective-permute-start.11 = (bf16[1280,256]{1,0:T(8,128)(2,1)S(1)}, bf16[1280,256]{1,0:T(8,128)(2,1)}, u32[]{:S(2)}, u32[]{:S(2)}) collective-permute-start(bf16[1280,256]{1,0:T(8,128)(2,1)S(1)} %add_convert_fusion.1), channel_id=1, source_target_pairs={{0,4},{1,5},{2,6},{3,7},{4,8},{5,9},{6,10},{7,11},{8,12},{9,13},{1... | collective-permute-start | bytes 1966088 | tf_op jit(solution)/shard_map/ppermute | solution.py:46
  94.9 38.1 %collective-permute-start.16 = (bf16[1280,128]{1,0:T(8,128)(2,1)}, bf16[1280,128]{1,0:T(8,128)(2,1)}, u32[]{:S(2)}, u32[]{:S(2)}) collective-permute-start(bf16[1280,128]{1,0:T(8,128)(2,1)} %add_convert_fusion.2), channel_id=1, source_target_pairs={{0,2},{1,3},{2,0},{3,1},{4,6},{5,7},{6,4},{7,5},{8,10},{9,11},{10,... | collective-permute-start | bytes 983048 | tf_op jit(solution)/shard_map/ppermute | solution.py:42
  105.2 14.1 %collective-permute-start.22 = (bf16[768,128]{1,0:T(8,128)(2,1)}, bf16[768,128]{1,0:T(8,128)(2,1)S(1)}, u32[]{:S(2)}, u32[]{:S(2)}) collective-permute-start(bf16[768,128]{1,0:T(8,128)(2,1)} %get-tuple-element.34), channel_id=1, source_target_pairs={{0,12},{1,13},{2,14},{3,15},{4,0},{5,1},{6,2},{7,3},{8,4},{9,5},{1... | collective-permute-start | bytes 589832 | tf_op jit(solution)/shard_map/ppermute | solution.py:46
  111.0 23.4 %collective-permute-start.12 = (bf16[1280,128]{1,0:T(8,128)(2,1)S(1)}, bf16[1280,128]{1,0:T(8,128)(2,1)S(1)}, u32[]{:S(2)}, u32[]{:S(2)}) collective-permute-start(bf16[1280,128]{1,0:T(8,128)(2,1)S(1)} %add_convert_fusion.3), channel_id=1, source_target_pairs={{0,2},{1,3},{2,0},{3,1},{4,6},{5,7},{6,4},{7,5},{8,10},{9,11},{10,... | collective-permute-start | bytes 983048 | tf_op jit(solution)/shard_map/ppermute | solution.py:42
  112.3 32.0 %all-to-all-start = ((f32[16,16,640]{2,1,0:T(8,128)}), f32[16,16,640]{2,1,0:T(8,128)S(1)}, u32[]{:S(2)}, u32[]{:S(2)}) async-start(f32[16,16,640]{2,1,0:T(8,128)} %get-tuple-element.35), calls=%async_computation | async-start | bytes 1310720 | tf_op jit(solution)/shard_map/all_to_all | solution.py:457
  116.0 16.1 %collective-permute-start.19 = (bf16[768,128]{1,0:T(8,128)(2,1)S(1)}, bf16[768,128]{1,0:T(8,128)(2,1)S(1)}, u32[]{:S(2)}, u32[]{:S(2)}) collective-permute-start(bf16[768,128]{1,0:T(8,128)(2,1)S(1)} %copy-done.25), channel_id=1, source_target_pairs={{0,4},{1,5},{2,6},{3,7},{4,8},{5,9},{6,10},{7,11},{8,12},{9,13},{1... | collective-permute-start | bytes 589832 | tf_op jit(solution)/shard_map/ppermute | solution.py:46
  118.0 17.1 %collective-permute-start.18 = (bf16[768,128]{1,0:T(8,128)(2,1)}, bf16[768,128]{1,0:T(8,128)(2,1)}, u32[]{:S(2)}, u32[]{:S(2)}) collective-permute-start(bf16[768,128]{1,0:T(8,128)(2,1)} %get-tuple-element.28), channel_id=1, source_target_pairs={{0,12},{1,13},{2,14},{3,15},{4,0},{5,1},{6,2},{7,3},{8,4},{9,5},{1... | collective-permute-start | bytes 589832 | tf_op jit(solution)/shard_map/ppermute | solution.py:46
  119.3 16.7 %collective-permute-start.21 = (bf16[768,128]{1,0:T(8,128)(2,1)}, bf16[768,128]{1,0:T(8,128)(2,1)}, u32[]{:S(2)}, u32[]{:S(2)}) collective-permute-start(bf16[768,128]{1,0:T(8,128)(2,1)} %get-tuple-element.32), channel_id=1, source_target_pairs={{0,4},{1,5},{2,6},{3,7},{4,8},{5,9},{6,10},{7,11},{8,12},{9,13},{1... | collective-permute-start | bytes 589832 | tf_op jit(solution)/shard_map/ppermute | solution.py:46
  134.4 28.4 %collective-permute-start.28 = (bf16[512,1024]{1,0:T(8,128)(2,1)S(1)}, bf16[512,1024]{1,0:T(8,128)(2,1)S(1)}, u32[]{:S(2)}, u32[]{:S(2)}) collective-permute-start(bf16[512,1024]{1,0:T(8,128)(2,1)S(1)} %copy-done.12), channel_id=1, source_target_pairs={{0,16},{1,17},{2,18},{3,19},{4,20},{5,21},{6,22},{7,23},{8,24},{9,... | collective-permute-start | bytes 3145736 | tf_op jit(solution)/shard_map/ppermute | solution.py:52
  135.1 45.1 %collective-permute-start.29 = (bf16[512,1024]{1,0:T(8,128)(2,1)S(1)}, bf16[512,1024]{1,0:T(8,128)(2,1)}, u32[]{:S(2)}, u32[]{:S(2)}) collective-permute-start(bf16[512,1024]{1,0:T(8,128)(2,1)S(1)} %copy-done.12), channel_id=1, source_target_pairs={{0,32},{1,33},{2,34},{3,35},{4,36},{5,37},{6,38},{7,39},{8,40},{9,... | collective-permute-start | bytes 3145736 | tf_op jit(solution)/shard_map/ppermute | solution.py:52
  136.0 48.2 %collective-permute-start.30 = (bf16[512,1024]{1,0:T(8,128)(2,1)S(1)}, bf16[512,1024]{1,0:T(8,128)(2,1)}, u32[]{:S(2)}, u32[]{:S(2)}) collective-permute-start(bf16[512,1024]{1,0:T(8,128)(2,1)S(1)} %copy-done.12), channel_id=1, source_target_pairs={{0,48},{1,49},{2,50},{3,51},{4,52},{5,53},{6,54},{7,55},{8,56},{9,... | collective-permute-start | bytes 3145736 | tf_op jit(solution)/shard_map/ppermute | solution.py:52
  144.1 12.3 %collective-permute-start.24 = (bf16[4096,128]{1,0:T(8,128)(2,1)}, bf16[4096,128]{1,0:T(8,128)(2,1)}, u32[]{:S(2)}, u32[]{:S(2)}) collective-permute-start(bf16[4096,128]{1,0:T(8,128)(2,1)} %finish_cache.1.mine), channel_id=1, source_target_pairs={{0,1},{1,0},{2,3},{3,2},{4,5},{5,4},{6,7},{7,6},{8,9},{9,8},{10,11... | collective-permute-start | bytes 3145736 | tf_op jit(solution)/shard_map/ppermute | solution.py:38
  161.3 23.0 %collective-permute-start.27 = (bf16[16,512]{1,0:T(8,128)(2,1)S(1)}, bf16[16,512]{1,0:T(8,128)(2,1)S(1)}, u32[]{:S(2)}, u32[]{:S(2)}) collective-permute-start(bf16[16,512]{1,0:T(8,128)(2,1)S(1)} %reshape.46.mine), channel_id=1, source_target_pairs={{0,64},{1,65},{2,66},{3,67},{4,68},{5,69},{6,70},{7,71},{8,72},{9,... | collective-permute-start | bytes 49160 | tf_op jit(solution)/shard_map/ppermute | solution.py:52
  (35 other events, 326.3 us)
where the time goes:
time: 222 us
  waiting for transfers between devices  83.8 us (38%)
  starting transfers between devices  48.6 us (22%)
  Pallas kernels  44.7 us (20%)
  blocking collectives  24.4 us (11%)
  other arithmetic  10.7 us (5%)
  local copies, waits for them, and re-layouts  8.45 us (4%)
    ppermute x11, waiting for transfers between devices, to_group(): return lax.ppermute(block, both, route(lambda f, t: (f ^ flip, t)))  36.2 us
    ppermute x12, waiting for transfers between devices, to_z(): lax.ppermute(block, both, route(lambda f, t: (f, ((t >> 2) + step) % 4 <<...  30.2 us
    all_to_all x1, blocking collectives, body(): lax.all_to_all(output, 'tp', 0, 0, tiled=True).astype(f32)  24.4 us
    ppermute x12, starting transfers between devices, to_z(): lax.ppermute(block, both, route(lambda f, t: (f, ((t >> 2) + step) % 4 <<...  18.8 us
    pallas_call x2, Pallas kernels, z_heads(): pl.pallas_call(z_kernel, out_shape=[jax.ShapeDtypeStruct((half, 2 * HD),...  17.7 us
    ppermute x11, starting transfers between devices, to_group(): return lax.ppermute(block, both, route(lambda f, t: (f ^ flip, t)))  13.5 us
    pallas_call x1, Pallas kernels, x_merge(): pl.pallas_call(x_merge_kernel, out_shape=[jax.ShapeDtypeStruct((half, HD)...  7.95 us
    ppermute x4, waiting for transfers between devices, to_core(): return lax.ppermute(block, both, route(lambda f, t: (f, t ^ 1)))  6.33 us
  transfers between devices with their start and end apart: 33, of which 15 were waited for; matrix products, arithmetic and copies ran while one was open for 6% of the time, Pallas kernels for 14%

commit v1 on v0

--- a/solution.py
+++ b/solution.py
@@ -1,5 +1,6 @@
 import jax
 import jax.numpy as jnp
+import numpy as np
 from jax import lax
 from jax.experimental import pallas as pl
 from jax.experimental.pallas import tpu as pltpu
@@ -113,8 +114,7 @@
 
 def x_merge_kernel(slots, x1, x2, *rest):
     messages, rest = rest[:N_FSDP], rest[N_FSDP:]
-    addend, w_query, w_keyvalue = rest[:3]
-    parts, (terms, merged, rows_ref) = rest[3:11], rest[11:]
+    addend, parts, merged = rest[0], rest[1:9], rest[9]
     i = pl.program_id(0)
 
     @pl.when(i == 0)
@@ -132,18 +132,12 @@
             for j in range(4):
                 parts[4 * side + j][...] = total[:, j * HD : (j + 1) * HD]
 
-    @pl.when(i == 1)
-    def _():
-        fresh_rows(slots[12], messages, w_query, w_keyvalue, terms, rows_ref)
-
-
-def fresh_rows(group, messages, w_query, w_keyvalue, out, rows_ref):
+
+def fresh_kernel(group, b0, b1, b2, b3, w_query, w_keyvalue, out, rows_ref):
+    beside = (b0, b1, b2, b3)
     for k in range(N_FSDP):
-        low = pl.multiple_of((group ^ k) * ROWS, ROWS)
-        for j in range(4):
-            rows_ref[pl.ds(low, ROWS), j * HD : (j + 1) * HD] = messages[k][
-                1024 + j * ROWS : 1024 + (j + 1) * ROWS, :
-            ]
+        low = pl.multiple_of((group[0] ^ k) * ROWS, ROWS)
+        rows_ref[pl.ds(low, ROWS), :] = beside[k & 3][k >> 2]
     rows = rows_ref[...]
     query = jnp.dot(rows, w_query[...], preferred_element_type=f32)
     keyvalue = jnp.dot(rows, w_keyvalue[...], preferred_element_type=f32)
@@ -152,6 +146,18 @@
             low = a * ROWS
             out[2 * a + h, :, :512] = query[low : low + ROWS, h * 512 : (h + 1) * 512]
             out[2 * a + h, :, 512:] = keyvalue[low : low + ROWS, h * HD : (h + 1) * HD]
+
+
+def fresh_terms(group, beside, w_query, w_keyvalue):
+    vmem = pl.BlockSpec(memory_space=pltpu.VMEM)
+    return pl.pallas_call(
+        fresh_kernel,
+        out_shape=jax.ShapeDtypeStruct((N_TP, ROWS, 640), f32),
+        in_specs=[pl.BlockSpec(memory_space=pltpu.SMEM)] + [vmem] * 6,
+        out_specs=vmem,
+        scratch_shapes=[pltpu.VMEM((N_FSDP * ROWS, 512), bf16)],
+        name="fresh_terms",
+    )(group, *beside, w_query, w_keyvalue)
 
 
 def whole(shape):
@@ -196,7 +202,7 @@
     )
 
 
-def x_heads(x1, x2, messages, slots, ready):
+def x_heads(x1, x2, messages, slots):
     count, depth = x1.shape
     rows = count - Z_FIRST
     half = rows // 2
@@ -206,62 +212,51 @@
         grid_spec=pltpu.PrefetchScalarGridSpec(
             num_scalar_prefetch=1,
             grid=(2,),
-            in_specs=[x_rows(depth, half)] * 2
-            + [whole(m.shape) for m in messages]
-            + [pl.BlockSpec(memory_space=pl.ANY)] * len(ready),
+            in_specs=[x_rows(depth, half)] * 2 + [whole(m.shape) for m in messages],
             out_specs=pl.BlockSpec((half, 4 * HD), lambda i, s: (i, 0)),
             scratch_shapes=[pltpu.VMEM((2 * depth, 4 * HD), bf16)],
         ),
         cost_estimate=cost(rows, depth),
         name="x_heads",
-    )(slots, x1, x2, *messages, *ready)
-
-
-def x_merge(x1, x2, messages, slots, addend, w_query, w_keyvalue):
+    )(slots, x1, x2, *messages)
+
+
+def x_merge(x1, x2, messages, slots, addend):
     count, depth = x1.shape
     rows = count - Z_FIRST
     half = rows // 2
-    terms = (N_TP, ROWS, 640)
     return pl.pallas_call(
         x_merge_kernel,
-        out_shape=[jax.ShapeDtypeStruct((half, HD), bf16)] * 8
-        + [jax.ShapeDtypeStruct(terms, f32)],
+        out_shape=[jax.ShapeDtypeStruct((half, HD), bf16)] * 8,
         grid_spec=pltpu.PrefetchScalarGridSpec(
             num_scalar_prefetch=1,
             grid=(2,),
             in_specs=[x_rows(depth, half)] * 2
             + [whole(m.shape) for m in messages]
-            + [pl.BlockSpec((half, 4 * HD), lambda i, s: (i, 0))]
-            + [whole(w_query.shape), whole(w_keyvalue.shape)],
-            out_specs=[whole((half, HD))] * 8 + [whole(terms)],
-            scratch_shapes=[
-                pltpu.VMEM((2 * depth, 4 * HD), bf16),
-                pltpu.VMEM((N_FSDP * ROWS, 512), bf16),
-            ],
+            + [pl.BlockSpec((half, 4 * HD), lambda i, s: (i, 0))],
+            out_specs=[whole((half, HD))] * 8,
+            scratch_shapes=[pltpu.VMEM((2 * depth, 4 * HD), bf16)],
         ),
         cost_estimate=cost(rows, depth),
         name="x_merge",
-    )(slots, x1, x2, *messages, addend, w_query, w_keyvalue)
-
-
-def message_kernel(kind, w_keyvalue, got, new_states, out):
+    )(slots, x1, x2, *messages, addend)
+
+
+def message_kernel(kind, w_keyvalue, got, out):
     depth = got.shape[0]
     out[:depth, :] = jnp.where(kind[0] == 0, w_keyvalue[:, :HD], w_keyvalue[:, HD:])
-    out[depth : 2 * depth, :] = got[...]
-    for j in range(4):
-        low = 2 * depth + j * ROWS
-        out[low : low + ROWS, :] = new_states[:, j * HD : (j + 1) * HD]
-
-
-def pack_message(kind, w_keyvalue, got, new_states):
+    out[depth:, :] = got[...]
+
+
+def pack_message(kind, w_keyvalue, got):
     vmem = pl.BlockSpec(memory_space=pltpu.VMEM)
     return pl.pallas_call(
         message_kernel,
-        out_shape=jax.ShapeDtypeStruct((2 * got.shape[0] + 4 * ROWS, HD), bf16),
-        in_specs=[pl.BlockSpec(memory_space=pltpu.SMEM)] + [vmem] * 3,
+        out_shape=jax.ShapeDtypeStruct((2 * got.shape[0], HD), bf16),
+        in_specs=[pl.BlockSpec(memory_space=pltpu.SMEM)] + [vmem] * 2,
         out_specs=vmem,
         name="pack_message",
-    )(kind, w_keyvalue, got, new_states)
+    )(kind, w_keyvalue, got)
 
 
 def output_kernel(group, mine, other, w0, w1, w2, w3, out):
@@ -286,35 +281,62 @@
     )(group, mine, other, *weights)
 
 
-def finish_kernel(*refs):
-    cosine, sine, out = refs[14:]
+def slot_table():
+    half = HD // 2
+    frequency = (theta_base ** (-2.0 * np.arange(half) / HD)).astype(np.float32)
+    angles = np.arange(L, dtype=np.float32)[:, None] * frequency[None, :]
+    angles = angles.astype(np.float64)
+    return np.concatenate([np.cos(angles), np.sin(angles)], axis=1).astype(np.float32)
+
+
+def finish_kernel(kind, *refs):
+    table, out = refs[14:]
     step = 256
-    base = 0
-    for addends in (refs[:4], refs[4:8], refs[8:11], refs[11:14]):
-        count = addends[0].shape[0]
-        for low in range(0, count, step):
-            rows = slice(low, low + step)
-            total = sum(ref[rows, :].astype(f32) for ref in addends)
-            at = base + low
-            table = slice(at % L, at % L + step)
-            total = total * cosine[table, :] + pltpu.roll(total, HD // 2, 1) * sine[table, :]
-            out[at : at + step, :] = total.astype(bf16)
-        base += count
-
-
-def finish_cache(pieces, cosine, sine):
-    arrays = [block for block, _, _ in pieces] + [cosine, sine]
+    lane = lax.broadcasted_iota(jnp.int32, (step, HD), 1)
+    lower = lane < HD // 2
+
+    def finish(rotated):
+        base = 0
+        for addends in (refs[:4], refs[4:8], refs[8:11], refs[11:14]):
+            count = addends[0].shape[0]
+            for low in range(0, count, step):
+                rows = slice(low, low + step)
+                total = sum(ref[rows, :].astype(f32) for ref in addends)
+                at = base + low
+                if rotated:
+                    angle = table[at % L : at % L + step, :]
+                    turned = pltpu.roll(angle, HD // 2, 1)
+                    cosine = jnp.where(lower, angle, turned)
+                    sine = jnp.where(lower, -turned, angle)
+                    total = total * cosine + pltpu.roll(total, HD // 2, 1) * sine
+                out[at : at + step, :] = total.astype(bf16)
+            base += count
+
+    @pl.when(kind[0] == 0)
+    def _():
+        finish(True)
+
+    @pl.when(kind[0] != 0)
+    def _():
+        finish(False)
+
+
+def finish_cache(kind, pieces, table):
+    arrays = [block for block, _, _ in pieces] + [table]
     specs = [
-        pl.BlockSpec((rows, HD), lambda i, at=at: at) for (_, rows, at) in pieces
-    ] + [pl.BlockSpec((L, HD), lambda i: (0, 0))] * 2
+        pl.BlockSpec((rows, HD), lambda i, s, at=at: at) for (_, rows, at) in pieces
+    ] + [whole((L, HD))]
     return pl.pallas_call(
         finish_kernel,
-        grid=(1,),
+        grid_spec=pltpu.PrefetchScalarGridSpec(
+            num_scalar_prefetch=1,
+            grid=(1,),
+            in_specs=specs,
+            out_specs=whole((NSEQ * L, HD)),
+        ),
         out_shape=jax.ShapeDtypeStruct((NSEQ * L, HD), bf16),
-        in_specs=specs,
-        out_specs=pl.BlockSpec((NSEQ * L, HD), lambda i: (0, 0)),
         name="finish_cache",
-    )(*arrays)
+    )(kind, *arrays)
 
 
 def attention_kernel(info, mine, other, fresh_mine, fresh_other, query, out):
@@ -409,18 +431,19 @@
     group = lax.axis_index("fsdp")
     me = lax.axis_index("tp")
     z, x, core = me >> 2, (me >> 1) & 1, me & 1
-    slots = prefix_states.shape[0]
     holds_keys = core == 0
 
     lower, upper = w_keyvalue[:, :HD], w_keyvalue[:, HD:]
     got = to_core(jnp.where(holds_keys, upper, lower))
     other_states = to_core(prefix_states)
     kind = core.reshape(1).astype(jnp.int32)
-    messages = relay(pack_message(kind, w_keyvalue, got, new_states))
-
-    slot_cos, slot_sin = tables(jnp.arange(L, dtype=f32))
-    slot_cos = jnp.where(holds_keys, slot_cos, 1.0)
-    slot_sin = jnp.where(holds_keys, slot_sin, 0.0)
+    new_pair = jnp.stack([new_states, to_group(new_states, 4)])
+    messages = relay(pack_message(kind, w_keyvalue, got))
+    new_rows = [new_pair]
+    for k in (1, 2, 3):
+        new_rows.append(to_group(new_pair, k))
+    own_group = group.reshape(1).astype(jnp.int32)
+    terms = fresh_terms(own_group, new_rows, w_query, w_keyvalue)
 
     def slot_of(z_step, x_flip):
         return (2 * ((z + z_step) % 4) + (x ^ x_flip)) ^ group
@@ -434,20 +457,18 @@
     first = picked(*far, *down, *far, *up, *((r, 1) for r in order))
     second = picked(*up, *own, *down, *own, *((r, 0) for r in order))
     states = (prefix_states, other_states, messages)
-    x_away = x_heads(*states, first, (slot_cos, slot_sin))
+    x_away = x_heads(*states, first)
     x_in = to_x(x_away)
     far_a, down_a, far_b, up_b = z_heads(*states, first)
     up_a, own_a, down_b, own_b = z_heads(*states, second)
     in_down_a, in_up_a, in_up_b, in_down_b = reduce_over_z(
         far_a, far_b, up_a, up_b, down_a, down_b
     )
-    *x_parts, terms = x_merge(*states, second, x_in, w_query, w_keyvalue)
+    x_parts = x_merge(*states, second, x_in)
     far_xa, up_xa, down_xa, own_xa, far_xb, up_xb, down_xb, own_xb = x_parts
     x_down_a, x_up_a, x_up_b, x_down_b = reduce_over_z(
         far_xa, far_xb, up_xa, up_xb, down_xa, down_xb
     )
-    half = Z_FIRST // 2
-    half_x = (slots - Z_FIRST) // 2
     x_in_a = to_x(add(own_a[:, HD:], in_down_a[:, HD:], in_up_a[:, HD:]))
     x_in_b = to_x(add(own_b[:, HD:], in_up_b[:, HD:], in_down_b[:, HD:]))
     outputs = [w_output]
@@ -455,7 +476,8 @@
         outputs.append(to_group(w_output, k))
 
     fresh = lax.all_to_all(terms, "tp", 0, 0, tiled=True)
-    fresh = transpose_mesh(jnp.sum(fresh, axis=0))
+    fresh = jnp.sum(fresh, axis=0)
+    fresh = transpose_mesh(fresh)
     seq_lengths = lengths[0]
     positions = (
         jnp.repeat(seq_lengths, STEPS) + jnp.tile(jnp.arange(STEPS, dtype=jnp.int32), NSEQ)
@@ -471,17 +493,19 @@
         .reshape(4 * ROWS, HD)
     )
 
+    half = Z_FIRST // 2
+    half_x = own_xa.shape[0]
     pieces = [(block, half, (0, 0)) for block in (own_a, in_down_a, in_up_a, x_in_a)]
     pieces += [(block, half, (0, 0)) for block in (own_b, in_up_b, in_down_b, x_in_b)]
     pieces += [(block, half_x, (0, 0)) for block in (own_xa, x_down_a, x_up_a)]
     pieces += [(block, half_x, (0, 0)) for block in (own_xb, x_up_b, x_down_b)]
-    cache_mine = finish_cache(pieces, slot_cos, slot_sin)
+    cache_mine = finish_cache(kind, pieces, jnp.asarray(slot_table()))
     cache_other = to_core(cache_mine)
     info = jnp.concatenate([seq_lengths, core.reshape(1).astype(jnp.int32)])
     attended = attend(info, cache_mine, cache_other, fresh_mine, fresh_other, query)
     attended = attended.reshape(ROWS, 512)
     beside = to_group(attended, 4)
-    output = output_terms(group.reshape(1).astype(jnp.int32), attended, beside, outputs)
+    output = output_terms(own_group, attended, beside, outputs)
     total = jnp.sum(lax.all_to_all(output, "tp", 0, 0, tiled=True).astype(f32), axis=0)
     mixed = output_owner(total.astype(bf16))
     return cache_mine, mixed

time: 222 us -> 215 us (0.968)
  waiting for transfers between devices: 83.8 us -> 71.5 us
  starting transfers between devices: 48.6 us -> 54.2 us
    ppermute x12, waiting for transfers between devices: 30.2 us -> 12.1 us  [to_z(): lax.ppermute(block, both, route(lambda f, t: (f, ((t >> 2) + step) % 4 <<...]
    ppermute x11 -> x15, starting transfers between devices: 13.5 us -> 18.7 us  [to_group(): return lax.ppermute(block, both, route(lambda f, t: (f ^ flip, t)))]
    ppermute x11 -> x15, waiting for transfers between devices: 36.2 us -> 41.3 us  [to_group(): return lax.ppermute(block, both, route(lambda f, t: (f ^ flip, t)))]
    pallas_call x1 -> x2, Pallas kernels: 4.02 us -> 6.86 us  [the longest x1 4.32 us: finish_cache(): pl.pallas_call(finish_kernel, grid_spec=pltpu.PrefetchScalarGridSpec(num_...]
    convert_element_type x6, other arithmetic: 4.8 us -> 7.47 us  [add(): return total.astype(bf16)]
    unnamed x53 -> x55, local copies, waits for them, and re-layouts: 6.14 us -> 5.05 us
  transfers between devices with their start and end apart: 33 -> 37, of which waited for: 15 -> 17; matrix products, arithmetic and copies ran while one was open for 6% -> 6% of each run, Pallas kernels for 14% -> 16%
where the time goes in v1:
time: 215 us; the launch traced here: 214 us
  waiting for transfers between devices  71.5 us (33%)
  starting transfers between devices  54.2 us (25%)
  Pallas kernels  46.4 us (22%)
  blocking collectives  23.1 us (11%)
  other arithmetic  10.9 us (5%)
  local copies, waits for them, and re-layouts  7.29 us (3%)
    ppermute x15, waiting for transfers between devices, to_group(): return lax.ppermute(block, both, route(lambda f, t: (f ^ flip, t)))  41.3 us
    all_to_all x1, blocking collectives, body(): lax.all_to_all(output, 'tp', 0, 0, tiled=True).astype(f32)  23.1 us
    ppermute x15, starting transfers between devices, to_group(): return lax.ppermute(block, both, route(lambda f, t: (f ^ flip, t)))  18.7 us
    pallas_call x2, Pallas kernels, z_heads(): pl.pallas_call(z_kernel, out_shape=[jax.ShapeDtypeStruct((half, 2 * HD),...  17.7 us
    ppermute x12, starting transfers between devices, to_z(): lax.ppermute(block, both, route(lambda f, t: (f, ((t >> 2) + step) % 4 <<...  17 us
    ppermute x12, waiting for transfers between devices, to_z(): lax.ppermute(block, both, route(lambda f, t: (f, ((t >> 2) + step) % 4 <<...  12.1 us
    convert_element_type x6, other arithmetic, add(): return total.astype(bf16)  7.47 us
    pallas_call x1, Pallas kernels, x_merge(): pl.pallas_call(x_merge_kernel, out_shape=[jax.ShapeDtypeStruct((half, HD)...  6.97 us
  transfers between devices with their start and end apart: 37, of which 17 were waited for; matrix products, arithmetic and copies ran while one was open for 6% of the time, Pallas kernels for 16%

profile of v1, /device:TPU:26, one launch (start us, length us, event | category | flops | bytes accessed | tf_op | source)
XLA Modules:
  0.0 214.3 jit_solution(7073832388308456626)
XLA Ops:
  2.3 6.0 %collective-permute-done.1.got = bf16[512,128]{1,0:T(8,128)(2,1)S(1)} collective-permute-done((bf16[512,128]{1,0:T(8,128)(2,1)S(1)}, bf16[512,128]{1,0:T(8,128)(2,1)S(1)}, u32[]{:S(2)}, u32[]{:S(2)}) %collective-permute-start.1) | collective-permute-done | bytes 131104 | tf_op jit(solution)/shard_map/ppermute | solution.py:39
  15.3 3.9 %collective-permute-done.5.rest_4_ = bf16[1024,128]{1,0:T(8,128)(2,1)S(1)} collective-permute-done((bf16[1024,128]{1,0:T(8,128)(2,1)}, bf16[1024,128]{1,0:T(8,128)(2,1)S(1)}, u32[]{:S(2)}, u32[]{:S(2)}) %collective-permute-start.5) | collective-permute-done | bytes 262176 | tf_op jit(solution)/shard_map/ppermute | solution.py:53
  22.2 2.9 %collective-permute-done.2.rest_1_ = bf16[1024,128]{1,0:T(8,128)(2,1)S(1)} collective-permute-done((bf16[1024,128]{1,0:T(8,128)(2,1)}, bf16[1024,128]{1,0:T(8,128)(2,1)S(1)}, u32[]{:S(2)}, u32[]{:S(2)}) %collective-permute-start.2) | collective-permute-done | bytes 262176 | tf_op jit(solution)/shard_map/ppermute | solution.py:53
  33.0 8.8 %z_heads.3 = (bf16[1280,256]{1,0:T(8,128)(2,1)}, bf16[1280,256]{1,0:T(8,128)(2,1)}, bf16[1280,256]{1,0:T(8,128)(2,1)}, bf16[1280,256]{1,0:T(8,128)(2,1)}) custom-call(s32[13]{0:T(128)} %stack.69.slots, bf16[4096,512]{1,0:T(8,128)(2,1)} %x1.7, bf16[4096,512]{1,0:T(8,128)(2,1)} %collective-permute-done.x2, bf16[1024,128]{1,0:T(8,128)(2,1)} %pack_message.1.rest_0_, ...), custom_call_target="tpu_custom_call" | custom-call | flops 2684354560 | bytes 7864320 | tf_op jit(solution)/shard_map/z_heads/pallas_call | solution.py:182
  41.8 4.0 %collective-permute-start.14 = (bf16[1280,256]{1,0:T(8,128)(2,1)}, bf16[1280,256]{1,0:T(8,128)(2,1)S(1)}, u32[]{:S(2)}, u32[]{:S(2)}) collective-permute-start(bf16[1280,256]{1,0:T(8,128)(2,1)} %get-tuple-element.25), channel_id=1, source_target_pairs={{0,12},{1,13},{2,14},{3,15},{4,0},{5,1},{6,2},{7,3},{8,4},{9,5},{1... | collective-permute-start | bytes 1966088 | tf_op jit(solution)/shard_map/ppermute | solution.py:47
  48.0 6.0 %x_heads.1 = bf16[1536,512]{1,0:T(8,128)(2,1)} custom-call(s32[13]{0:T(128)} %stack.69.slots, bf16[4096,512]{1,0:T(8,128)(2,1)} %x1.7, bf16[4096,512]{1,0:T(8,128)(2,1)} %collective-permute-done.x2, bf16[1024,128]{1,0:T(8,128)(2,1)} %pack_message.1.rest_0_, bf16[1024,128]{1,0:T(8,128)(2,1)} %copy-done.2, bf16[1024,128]{1,0:T(8,128)(2,1)} %copy-done.1, ...), custom_call_target="tpu_custom_call" | custom-call | flops 1610612736 | bytes 4718592 | tf_op jit(solution)/shard_map/x_heads/pallas_call | solution.py:209
  56.1 8.9 %z_heads.2 = (bf16[1280,256]{1,0:T(8,128)(2,1)}, bf16[1280,256]{1,0:T(8,128)(2,1)}, bf16[1280,256]{1,0:T(8,128)(2,1)}, bf16[1280,256]{1,0:T(8,128)(2,1)}) custom-call(s32[13]{0:T(128)} %stack.67.slots, bf16[4096,512]{1,0:T(8,128)(2,1)} %x1.7, bf16[4096,512]{1,0:T(8,128)(2,1)} %collective-permute-done.x2, bf16[1024,128]{1,0:T(8,128)(2,1)} %pack_message.1.rest_0_, ...), custom_call_target="tpu_custom_call" | custom-call | flops 2684354560 | bytes 7864320 | tf_op jit(solution)/shard_map/z_heads/pallas_call | solution.py:182
  67.2 3.2 %collective-permute-start.15 = (bf16[1280,256]{1,0:T(8,128)(2,1)}, bf16[1280,256]{1,0:T(8,128)(2,1)}, u32[]{:S(2)}, u32[]{:S(2)}) collective-permute-start(bf16[1280,256]{1,0:T(8,128)(2,1)} %add_convert_fusion), channel_id=1, source_target_pairs={{0,12},{1,13},{2,14},{3,15},{4,0},{5,1},{6,2},{7,3},{8,4},{9,5},{1... | collective-permute-start | bytes 1966088 | tf_op jit(solution)/shard_map/ppermute | solution.py:47
  75.2 3.0 %collective-permute-start.27 = (bf16[2,16,512]{2,1,0:T(8,128)(2,1)S(1)}, bf16[2,16,512]{2,1,0:T(8,128)(2,1)S(1)}, u32[]{:S(2)}, u32[]{:S(2)}) collective-permute-start(bf16[2,16,512]{2,1,0:T(8,128)(2,1)S(1)} %pad_maximum_fusion.b0), channel_id=1, source_target_pairs={{0,32},{1,33},{2,34},{3,35},{4,36},{5,37},{6,38},{7,39},{8,40},{9,... | collective-permute-start | bytes 98312 | tf_op jit(solution)/shard_map/ppermute | solution.py:53
  78.2 9.0 %collective-permute-done.10 = bf16[1280,256]{1,0:T(8,128)(2,1)S(1)} collective-permute-done((bf16[1280,256]{1,0:T(8,128)(2,1)}, bf16[1280,256]{1,0:T(8,128)(2,1)S(1)}, u32[]{:S(2)}, u32[]{:S(2)}) %collective-permute-start.10) | collective-permute-done | bytes 655392 | tf_op jit(solution)/shard_map/ppermute | solution.py:47
  88.5 3.8 %collective-permute-done.28.b3 = bf16[2,16,512]{2,1,0:T(8,128)(2,1)S(1)} collective-permute-done((bf16[2,16,512]{2,1,0:T(8,128)(2,1)S(1)}, bf16[2,16,512]{2,1,0:T(8,128)(2,1)S(1)}, u32[]{:S(2)}, u32[]{:S(2)}) %collective-permute-start.28) | collective-permute-done | bytes 32800 | tf_op jit(solution)/shard_map/ppermute | solution.py:53
  95.5 4.9 %all-to-all-start = ((f32[16,16,640]{2,1,0:T(8,128)}), f32[16,16,640]{2,1,0:T(8,128)S(1)}, u32[]{:S(2)}, u32[]{:S(2)}) async-start(f32[16,16,640]{2,1,0:T(8,128)} %fresh_terms.1), calls=%async_computation | async-start | bytes 1310720 | tf_op jit(solution)/shard_map/all_to_all | solution.py:478
  102.5 3.4 %collective-permute-start.16 = (bf16[1280,128]{1,0:T(8,128)(2,1)}, bf16[1280,128]{1,0:T(8,128)(2,1)}, u32[]{:S(2)}, u32[]{:S(2)}) collective-permute-start(bf16[1280,128]{1,0:T(8,128)(2,1)} %add_convert_fusion.2), channel_id=1, source_target_pairs={{0,2},{1,3},{2,0},{3,1},{4,6},{5,7},{6,4},{7,5},{8,10},{9,11},{10,... | collective-permute-start | bytes 983048 | tf_op jit(solution)/shard_map/ppermute | solution.py:43
  107.1 7.0 %x_merge.1 = (bf16[768,128]{1,0:T(8,128)(2,1)}, bf16[768,128]{1,0:T(8,128)(2,1)}, bf16[768,128]{1,0:T(8,128)(2,1)}, bf16[768,128]{1,0:T(8,128)(2,1)}, bf16[768,1...) custom-call(s32[13]{0:T(128)} %stack.67.slots, ...), custom_call_target="tpu_custom_call" | custom-call | flops 1610612736 | bytes 4718592 | tf_op jit(solution)/shard_map/x_merge/pallas_call | solution.py:228
  118.7 3.2 %collective-permute-start.18 = (bf16[768,128]{1,0:T(8,128)(2,1)}, bf16[768,128]{1,0:T(8,128)(2,1)}, u32[]{:S(2)}, u32[]{:S(2)}) collective-permute-start(bf16[768,128]{1,0:T(8,128)(2,1)} %get-tuple-element.27), channel_id=1, source_target_pairs={{0,12},{1,13},{2,14},{3,15},{4,0},{5,1},{6,2},{7,3},{8,4},{9,5},{1... | collective-permute-start | bytes 589832 | tf_op jit(solution)/shard_map/ppermute | solution.py:47
  134.7 4.3 %finish_cache.1.mine = bf16[4096,128]{1,0:T(8,128)(2,1)} custom-call(s32[1]{0:T(128)} %bitcast.kind, bf16[1280,256]{1,0:T(8,128)(2,1)} %get-tuple-element.18.refs_0_, bf16[1280,256]{1,0:T(8,128)(2,1)} %collective-permute-done.9.refs_1_, bf16[1280,256]{1,0:T(8,128)(2,1)} %collective-permute-done.11.refs_2_, bf16[1280,128]{1,0:T(8,128)(2,1)} %copy-done.14, ...), custom_call_target="tpu_custom_call" | custom-call | tf_op jit(solution)/shard_map/finish_cache/pallas_call | solution.py:329
  139.2 3.9 %collective-permute-start.29 = (f32[16,640]{1,0:T(8,128)S(1)}, f32[16,640]{1,0:T(8,128)S(1)}, u32[]{:S(2)}, u32[]{:S(2)}) collective-permute-start(f32[16,640]{1,0:T(8,128)S(1)} %reduce_sum.21), channel_id=1, source_target_pairs={{0,0},{1,1},{2,16},{3,17},{4,32},{5,33},{6,48},{7,49},{8,64},{9,65... | collective-permute-start | bytes 122888 | tf_op jit(solution)/shard_map/ppermute | solution.py:57
  143.7 6.5 %collective-permute-done.29 = f32[16,640]{1,0:T(8,128)S(1)} collective-permute-done((f32[16,640]{1,0:T(8,128)S(1)}, f32[16,640]{1,0:T(8,128)S(1)}, u32[]{:S(2)}, u32[]{:S(2)}) %collective-permute-start.29) | collective-permute-done | bytes 40992 | tf_op jit(solution)/shard_map/ppermute | solution.py:57
  152.2 3.5 %attend.1 = bf16[64,128]{1,0:T(8,128)(2,1)} custom-call(s32[5]{0:T(128)} %pad_add_fusion.info, bf16[4096,128]{1,0:T(8,128)(2,1)} %finish_cache.1.mine, bf16[4096,128]{1,0:T(8,128)(2,1)} %collective-permute-done.24.other, bf16[16,128]{1,0:T(8,128)(2,1)} %copy-done.23, bf16[16,128]{1,0:T(8,128)(2,1)} %copy-done.25, bf16[64,128]{1,0:T(8,128)(2,1)} %fusion.1.query), custom_call_target="tpu_custom_call" | custom-call | tf_op jit(solution)/shard_map/attend/pallas_call | solution.py:379
  157.1 17.8 %collective-permute-done.33.w2 = bf16[512,1024]{1,0:T(8,128)(2,1)} collective-permute-done((bf16[512,1024]{1,0:T(8,128)(2,1)S(1)}, bf16[512,1024]{1,0:T(8,128)(2,1)}, u32[]{:S(2)}, u32[]{:S(2)}) %collective-permute-start.33) | collective-permute-done | bytes 1048608 | tf_op jit(solution)/shard_map/ppermute | solution.py:53
  175.0 3.3 %collective-permute-done.34.w3 = bf16[512,1024]{1,0:T(8,128)(2,1)} collective-permute-done((bf16[512,1024]{1,0:T(8,128)(2,1)S(1)}, bf16[512,1024]{1,0:T(8,128)(2,1)}, u32[]{:S(2)}, u32[]{:S(2)}) %collective-permute-start.34) | collective-permute-done | bytes 1048608 | tf_op jit(solution)/shard_map/ppermute | solution.py:53
  178.8 3.7 %output_terms.1 = bf16[16,16,512]{2,1,0:T(8,128)(2,1)} custom-call(s32[1]{0:T(128)} %bitcast.8.group, bf16[16,512]{1,0:T(8,128)(2,1)} %copy-done.18, bf16[16,512]{1,0:T(8,128)(2,1)} %copy-done.22, bf16[512,1024]{1,0:T(8,128)(2,1)} %w0.1, bf16[512,1024]{1,0:T(8,128)(2,1)} %copy-done.12, bf16[512,1024]{1,0:T(8,128)(2,1)} %collective-permute-done.33.w2, ...), custom_call_target="tpu_custom_call" | custom-call | tf_op jit(solution)/shard_map/output_terms/pallas_call | solution.py:275
  182.6 23.1 %all_to_all.10 = bf16[16,16,512]{2,1,0:T(8,128)(2,1)S(1)} all-to-all(bf16[16,16,512]{2,1,0:T(8,128)(2,1)} %output_terms.1), channel_id=1, replica_groups=mesh['fsdp'=8,'tp'=16] {'tp'}, dimensions={0} | all-to-all | bytes 524288 | tf_op jit(solution)/shard_map/all_to_all | solution.py:509
  208.5 5.2 %collective-permute-done.35 = bf16[16,512]{1,0:T(8,128)(2,1)S(1)} collective-permute-done((bf16[16,512]{1,0:T(8,128)(2,1)S(1)}, bf16[16,512]{1,0:T(8,128)(2,1)S(1)}, u32[]{:S(2)}, u32[]{:S(2)}) %collective-permute-start.35) | collective-permute-done | bytes 16416 | tf_op jit(solution)/shard_map/ppermute | solution.py:61
  (142 shorter events, 64.0 us)
Async XLA Ops:
  0.6 31.6 %collective-permute-start = (bf16[4096,512]{1,0:T(8,128)(2,1)}, bf16[4096,512]{1,0:T(8,128)(2,1)}, u32[]{:S(2)}, u32[]{:S(2)}) collective-permute-start(bf16[4096,512]{1,0:T(8,128)(2,1)} %x1.7), channel_id=1, source_target_pairs={{0,1},{1,0},{2,3},{3,2},{4,5},{5,4},{6,7},{7,6},{8,9},{9,8},{10,11... | collective-permute-start | bytes 12582920 | tf_op jit(solution)/shard_map/ppermute | solution.py:39
  11.2 10.9 %collective-permute-start.3 = (bf16[1024,128]{1,0:T(8,128)(2,1)}, bf16[1024,128]{1,0:T(8,128)(2,1)S(1)}, u32[]{:S(2)}, u32[]{:S(2)}) collective-permute-start(bf16[1024,128]{1,0:T(8,128)(2,1)} %pack_message.1.rest_0_), channel_id=1, source_target_pairs={{0,32},{1,33},{2,34},{3,35},{4,36},{5,37},{6,38},{7,39},{8,40},{9,... | collective-permute-start | bytes 786440 | tf_op jit(solution)/shard_map/ppermute | solution.py:53
  12.4 12.7 %collective-permute-start.2 = (bf16[1024,128]{1,0:T(8,128)(2,1)}, bf16[1024,128]{1,0:T(8,128)(2,1)S(1)}, u32[]{:S(2)}, u32[]{:S(2)}) collective-permute-start(bf16[1024,128]{1,0:T(8,128)(2,1)} %pack_message.1.rest_0_), channel_id=1, source_target_pairs={{0,16},{1,17},{2,18},{3,19},{4,20},{5,21},{6,22},{7,23},{8,24},{9,... | collective-permute-start | bytes 786440 | tf_op jit(solution)/shard_map/ppermute | solution.py:53
  12.4 14.9 %collective-permute-start.4 = (bf16[1024,128]{1,0:T(8,128)(2,1)}, bf16[1024,128]{1,0:T(8,128)(2,1)S(1)}, u32[]{:S(2)}, u32[]{:S(2)}) collective-permute-start(bf16[1024,128]{1,0:T(8,128)(2,1)} %pack_message.1.rest_0_), channel_id=1, source_target_pairs={{0,48},{1,49},{2,50},{3,51},{4,52},{5,53},{6,54},{7,55},{8,56},{9,... | collective-permute-start | bytes 786440 | tf_op jit(solution)/shard_map/ppermute | solution.py:53
  19.2 10.5 %collective-permute-start.6 = (bf16[1024,128]{1,0:T(8,128)(2,1)S(1)}, bf16[1024,128]{1,0:T(8,128)(2,1)S(1)}, u32[]{:S(2)}, u32[]{:S(2)}) collective-permute-start(bf16[1024,128]{1,0:T(8,128)(2,1)S(1)} %collective-permute-done.5.rest_4_), channel_id=1, source_target_pairs={{0,16},{1,17},{2,18},{3,19},{4,20},{5,21},{6,22},{7,23},{8,24},{9,... | collective-permute-start | bytes 786440 | tf_op jit(solution)/shard_map/ppermute | solution.py:53
  41.8 23.2 %collective-permute-start.14 = (bf16[1280,256]{1,0:T(8,128)(2,1)}, bf16[1280,256]{1,0:T(8,128)(2,1)S(1)}, u32[]{:S(2)}, u32[]{:S(2)}) collective-permute-start(bf16[1280,256]{1,0:T(8,128)(2,1)} %get-tuple-element.25), channel_id=1, source_target_pairs={{0,12},{1,13},{2,14},{3,15},{4,0},{5,1},{6,2},{7,3},{8,4},{9,5},{1... | collective-permute-start | bytes 1966088 | tf_op jit(solution)/shard_map/ppermute | solution.py:47
  45.9 24.5 %collective-permute-start.25 = (bf16[16,512]{1,0:T(8,128)(2,1)S(1)}, bf16[16,512]{1,0:T(8,128)(2,1)}, u32[]{:S(2)}, u32[]{:S(2)}) collective-permute-start(bf16[16,512]{1,0:T(8,128)(2,1)S(1)} %copy-done.24), channel_id=1, source_target_pairs={{0,64},{1,65},{2,66},{3,67},{4,68},{5,69},{6,70},{7,71},{8,72},{9,... | collective-permute-start | bytes 49160 | tf_op jit(solution)/shard_map/ppermute | solution.py:53
  54.0 51.9 %collective-permute-start.17 = (bf16[1536,512]{1,0:T(8,128)(2,1)}, bf16[1536,512]{1,0:T(8,128)(2,1)S(1)}, u32[]{:S(2)}, u32[]{:S(2)}) collective-permute-start(bf16[1536,512]{1,0:T(8,128)(2,1)} %x_heads.1), channel_id=1, source_target_pairs={{0,2},{1,3},{2,0},{3,1},{4,6},{5,7},{6,4},{7,5},{8,10},{9,11},{10,... | collective-permute-start | bytes 4718600 | tf_op jit(solution)/shard_map/ppermute | solution.py:43
  56.1 44.2 %collective-permute-start.13 = (bf16[1280,256]{1,0:T(8,128)(2,1)}, bf16[1280,256]{1,0:T(8,128)(2,1)S(1)}, u32[]{:S(2)}, u32[]{:S(2)}) collective-permute-start(bf16[1280,256]{1,0:T(8,128)(2,1)} %get-tuple-element.23), channel_id=1, source_target_pairs={{0,4},{1,5},{2,6},{3,7},{4,8},{5,9},{6,10},{7,11},{8,12},{9,13},{1... | collective-permute-start | bytes 1966088 | tf_op jit(solution)/shard_map/ppermute | solution.py:47
  56.1 31.1 %collective-permute-start.10 = (bf16[1280,256]{1,0:T(8,128)(2,1)}, bf16[1280,256]{1,0:T(8,128)(2,1)S(1)}, u32[]{:S(2)}, u32[]{:S(2)}) collective-permute-start(bf16[1280,256]{1,0:T(8,128)(2,1)} %get-tuple-element.21), channel_id=1, source_target_pairs={{0,4},{1,5},{2,6},{3,7},{4,8},{5,9},{6,10},{7,11},{8,12},{9,13},{1... | collective-permute-start | bytes 1966088 | tf_op jit(solution)/shard_map/ppermute | solution.py:47
  67.2 33.2 %collective-permute-start.15 = (bf16[1280,256]{1,0:T(8,128)(2,1)}, bf16[1280,256]{1,0:T(8,128)(2,1)}, u32[]{:S(2)}, u32[]{:S(2)}) collective-permute-start(bf16[1280,256]{1,0:T(8,128)(2,1)} %add_convert_fusion), channel_id=1, source_target_pairs={{0,12},{1,13},{2,14},{3,15},{4,0},{5,1},{6,2},{7,3},{8,4},{9,5},{1... | collective-permute-start | bytes 1966088 | tf_op jit(solution)/shard_map/ppermute | solution.py:47
  75.2 13.3 %collective-permute-start.27 = (bf16[2,16,512]{2,1,0:T(8,128)(2,1)S(1)}, bf16[2,16,512]{2,1,0:T(8,128)(2,1)S(1)}, u32[]{:S(2)}, u32[]{:S(2)}) collective-permute-start(bf16[2,16,512]{2,1,0:T(8,128)(2,1)S(1)} %pad_maximum_fusion.b0), channel_id=1, source_target_pairs={{0,32},{1,33},{2,34},{3,35},{4,36},{5,37},{6,38},{7,39},{8,40},{9,... | collective-permute-start | bytes 98312 | tf_op jit(solution)/shard_map/ppermute | solution.py:53
  88.5 28.4 %collective-permute-start.9 = (bf16[1280,256]{1,0:T(8,128)(2,1)}, bf16[1280,256]{1,0:T(8,128)(2,1)}, u32[]{:S(2)}, u32[]{:S(2)}) collective-permute-start(bf16[1280,256]{1,0:T(8,128)(2,1)} %get-tuple-element.19), channel_id=1, source_target_pairs={{0,12},{1,13},{2,14},{3,15},{4,0},{5,1},{6,2},{7,3},{8,4},{9,5},{1... | collective-permute-start | bytes 1966088 | tf_op jit(solution)/shard_map/ppermute | solution.py:47
  92.3 24.5 %collective-permute-start.11 = (bf16[1280,256]{1,0:T(8,128)(2,1)}, bf16[1280,256]{1,0:T(8,128)(2,1)}, u32[]{:S(2)}, u32[]{:S(2)}) collective-permute-start(bf16[1280,256]{1,0:T(8,128)(2,1)} %add_convert_fusion.1), channel_id=1, source_target_pairs={{0,4},{1,5},{2,6},{3,7},{4,8},{5,9},{6,10},{7,11},{8,12},{9,13},{1... | collective-permute-start | bytes 1966088 | tf_op jit(solution)/shard_map/ppermute | solution.py:47
  95.5 43.7 %all-to-all-start = ((f32[16,16,640]{2,1,0:T(8,128)}), f32[16,16,640]{2,1,0:T(8,128)S(1)}, u32[]{:S(2)}, u32[]{:S(2)}) async-start(f32[16,16,640]{2,1,0:T(8,128)} %fresh_terms.1), calls=%async_computation | async-start | bytes 1310720 | tf_op jit(solution)/shard_map/all_to_all | solution.py:478
  102.5 25.1 %collective-permute-start.16 = (bf16[1280,128]{1,0:T(8,128)(2,1)}, bf16[1280,128]{1,0:T(8,128)(2,1)}, u32[]{:S(2)}, u32[]{:S(2)}) collective-permute-start(bf16[1280,128]{1,0:T(8,128)(2,1)} %add_convert_fusion.2), channel_id=1, source_target_pairs={{0,2},{1,3},{2,0},{3,1},{4,6},{5,7},{6,4},{7,5},{8,10},{9,11},{10,... | collective-permute-start | bytes 983048 | tf_op jit(solution)/shard_map/ppermute | solution.py:43
  118.1 11.8 %collective-permute-start.12 = (bf16[1280,128]{1,0:T(8,128)(2,1)S(1)}, bf16[1280,128]{1,0:T(8,128)(2,1)S(1)}, u32[]{:S(2)}, u32[]{:S(2)}) collective-permute-start(bf16[1280,128]{1,0:T(8,128)(2,1)S(1)} %add_convert_fusion.3), channel_id=1, source_target_pairs={{0,2},{1,3},{2,0},{3,1},{4,6},{5,7},{6,4},{7,5},{8,10},{9,11},{10,... | collective-permute-start | bytes 983048 | tf_op jit(solution)/shard_map/ppermute | solution.py:43
  118.7 11.2 %collective-permute-start.18 = (bf16[768,128]{1,0:T(8,128)(2,1)}, bf16[768,128]{1,0:T(8,128)(2,1)}, u32[]{:S(2)}, u32[]{:S(2)}) collective-permute-start(bf16[768,128]{1,0:T(8,128)(2,1)} %get-tuple-element.27), channel_id=1, source_target_pairs={{0,12},{1,13},{2,14},{3,15},{4,0},{5,1},{6,2},{7,3},{8,4},{9,5},{1... | collective-permute-start | bytes 589832 | tf_op jit(solution)/shard_map/ppermute | solution.py:47
  129.8 27.3 %collective-permute-start.32 = (bf16[512,1024]{1,0:T(8,128)(2,1)S(1)}, bf16[512,1024]{1,0:T(8,128)(2,1)S(1)}, u32[]{:S(2)}, u32[]{:S(2)}) collective-permute-start(bf16[512,1024]{1,0:T(8,128)(2,1)S(1)} %copy-done.11), channel_id=1, source_target_pairs={{0,16},{1,17},{2,18},{3,19},{4,20},{5,21},{6,22},{7,23},{8,24},{9,... | collective-permute-start | bytes 3145736 | tf_op jit(solution)/shard_map/ppermute | solution.py:53
  129.9 45.0 %collective-permute-start.33 = (bf16[512,1024]{1,0:T(8,128)(2,1)S(1)}, bf16[512,1024]{1,0:T(8,128)(2,1)}, u32[]{:S(2)}, u32[]{:S(2)}) collective-permute-start(bf16[512,1024]{1,0:T(8,128)(2,1)S(1)} %copy-done.11), channel_id=1, source_target_pairs={{0,32},{1,33},{2,34},{3,35},{4,36},{5,37},{6,38},{7,39},{8,40},{9,... | collective-permute-start | bytes 3145736 | tf_op jit(solution)/shard_map/ppermute | solution.py:53
  131.8 46.4 %collective-permute-start.34 = (bf16[512,1024]{1,0:T(8,128)(2,1)S(1)}, bf16[512,1024]{1,0:T(8,128)(2,1)}, u32[]{:S(2)}, u32[]{:S(2)}) collective-permute-start(bf16[512,1024]{1,0:T(8,128)(2,1)S(1)} %copy-done.11), channel_id=1, source_target_pairs={{0,48},{1,49},{2,50},{3,51},{4,52},{5,53},{6,54},{7,55},{8,56},{9,... | collective-permute-start | bytes 3145736 | tf_op jit(solution)/shard_map/ppermute | solution.py:53
  139.1 12.5 %collective-permute-start.24 = (bf16[4096,128]{1,0:T(8,128)(2,1)}, bf16[4096,128]{1,0:T(8,128)(2,1)}, u32[]{:S(2)}, u32[]{:S(2)}) collective-permute-start(bf16[4096,128]{1,0:T(8,128)(2,1)} %finish_cache.1.mine), channel_id=1, source_target_pairs={{0,1},{1,0},{2,3},{3,2},{4,5},{5,4},{6,7},{7,6},{8,9},{9,8},{10,11... | collective-permute-start | bytes 3145736 | tf_op jit(solution)/shard_map/ppermute | solution.py:39
  139.2 10.9 %collective-permute-start.29 = (f32[16,640]{1,0:T(8,128)S(1)}, f32[16,640]{1,0:T(8,128)S(1)}, u32[]{:S(2)}, u32[]{:S(2)}) collective-permute-start(f32[16,640]{1,0:T(8,128)S(1)} %reduce_sum.21), channel_id=1, source_target_pairs={{0,0},{1,1},{2,16},{3,17},{4,32},{5,33},{6,48},{7,49},{8,64},{9,65... | collective-permute-start | bytes 122888 | tf_op jit(solution)/shard_map/ppermute | solution.py:57
  156.5 21.8 %collective-permute-start.31 = (bf16[16,512]{1,0:T(8,128)(2,1)S(1)}, bf16[16,512]{1,0:T(8,128)(2,1)S(1)}, u32[]{:S(2)}, u32[]{:S(2)}) collective-permute-start(bf16[16,512]{1,0:T(8,128)(2,1)S(1)} %reshape.46.mine), channel_id=1, source_target_pairs={{0,64},{1,65},{2,66},{3,67},{4,68},{5,69},{6,70},{7,71},{8,72},{9,... | collective-permute-start | bytes 49160 | tf_op jit(solution)/shard_map/ppermute | solution.py:53
  (40 other events, 351.2 us)
